TPU v7x, 32 devices: a whole 2x2x4 slice. The times are simulated.
32 devices in a mesh: expert: 2 (over x), dp: 16 (over z, y, core).
Axes of the slice: x: 2, y: 2, z: 4, core: 2. Of those that a mesh axis runs over, the one named last changes fastest.
Arguments:
- tokens: bfloat16 [4096, 3072], P(('expert', 'dp')), may hold values from -6 to 6
- out_grad: bfloat16 [4096, 3072], P(('expert', 'dp')), may hold values from -6 to 6
- routes: int32 [4096, 2], P(('expert', 'dp')), may hold values from 0 to 7, all different within a row; in each aligned block of 128 rows (0 to 127, 128 to 255, ...) at most 40 rows name the same one
- gates: float32 [4096, 2], P(('expert', 'dp')), may hold values from 0.2 to 1
- w_gate: bfloat16 [8, 3072, 128], P('expert', 'dp'), may hold values from -0.109375 to 0.109375
- w_up: bfloat16 [8, 3072, 128], P('expert', 'dp'), may hold values from -0.109375 to 0.109375
- w_down_t: bfloat16 [8, 3072, 128], P('expert', 'dp'), may hold values from -0.5 to 0.5
Outputs:
- token_grad: bfloat16 [4096, 3072], P(('expert', 'dp'))
- grad_gate: float32 [8, 3072, 128], P('expert', 'dp')
- grad_up: float32 [8, 3072, 128], P('expert', 'dp')
Inputs may be any that keep to these rules, and one draw needn't show every extreme that they name: `routes`: each row names two different experts. No expert is named by more than 40 of the rows of one device, and in every draw some device names some expert exactly 40 times.
All inputs are finite; a program needn't handle non-finite values.
Results may differ from a plain program's by a relative error of at most 0.0065.
Values may be sent and summed in bfloat16 or wider, within the bound.
A program may use at most 64 MiB of HBM per device.

v0:
```python
import math

import jax
import jax.numpy as jnp
from jax import lax
from jax.sharding import PartitionSpec as P

EXPERTS = 8
CAP = 40


def local(tokens, out_grad, routes, gates, w_gate, w_up, w_down_t):
    tok_rows, model_width = tokens.shape
    n_expert = lax.axis_size("expert")
    n_data = lax.axis_size("dp")
    local_count = w_gate.shape[0]
    hidden = w_gate.shape[2]
    slot_count = EXPERTS * CAP
    flat_routes = routes.reshape(-1)
    onehot = (flat_routes[:, None] == jnp.arange(EXPERTS, dtype=jnp.int32)[None, :]).astype(
        jnp.int32
    )
    rank_rows = jnp.cumsum(onehot, axis=0) - 1
    position = jnp.sum(rank_rows * onehot, axis=1)
    slot_token = (flat_routes * CAP + position).reshape(tok_rows, 2)
    chosen = jnp.arange(slot_count, dtype=jnp.int32)[:, None, None] == slot_token[None, :, :]
    dispatch = jnp.any(chosen, axis=2).astype(jnp.bfloat16)
    slot_gate = jnp.sum(jnp.where(chosen, gates[None, :, :], 0.0), axis=(1, 2))
    rows_out = jnp.dot(dispatch, tokens, preferred_element_type=jnp.float32).astype(jnp.bfloat16)
    grads_out = (
        jnp.dot(dispatch, out_grad, preferred_element_type=jnp.float32) * slot_gate[:, None]
    ).astype(jnp.bfloat16)
    rows_out = rows_out.reshape(n_expert, local_count * CAP, model_width)
    grads_out = grads_out.reshape(n_expert, local_count * CAP, model_width)
    wg_full, wu_full, wd_full = (
        lax.all_gather(w_gate, "dp", axis=1, tiled=True),
        lax.all_gather(w_up, "dp", axis=1, tiled=True),
        lax.all_gather(w_down_t, "dp", axis=1, tiled=True),
    )
    rows_in, grads_in = (
        lax.all_to_all(rows_out, "expert", split_axis=0, concat_axis=0, tiled=True),
        lax.all_to_all(grads_out, "expert", split_axis=0, concat_axis=0, tiled=True),
    )
    rows_in = rows_in.reshape(n_expert, local_count, CAP, model_width)
    grads_in = grads_in.reshape(n_expert, local_count, CAP, model_width)
    in_weights = jnp.concatenate([wg_full, wu_full], axis=2)
    gate_up = jnp.einsum("sxcd,xdf->sxcf", rows_in, in_weights, preferred_element_type=jnp.float32)
    gate_pre = gate_up[..., :hidden]
    up_pre = gate_up[..., hidden:]
    sigmoid_gate = jax.nn.sigmoid(gate_pre)
    silu_gate = gate_pre * sigmoid_gate
    act_grad = jnp.einsum("sxcd,xdf->sxcf", grads_in, wd_full, preferred_element_type=jnp.float32)
    gate_grad = act_grad * up_pre * sigmoid_gate * (1.0 + gate_pre * (1.0 - sigmoid_gate))
    up_grad = act_grad * silu_gate
    hidden_grad = jnp.concatenate([gate_grad, up_grad], axis=3).astype(jnp.bfloat16)
    slot_input = jnp.einsum(
        "sxcf,xdf->sxcd", hidden_grad, in_weights, preferred_element_type=jnp.float32
    ).astype(jnp.bfloat16)
    returned = lax.all_to_all(
        slot_input.reshape(n_expert, local_count * CAP, model_width),
        "expert",
        split_axis=0,
        concat_axis=0,
        tiled=True,
    )
    returned = returned.reshape(slot_count, model_width)
    token_grad = jnp.einsum(
        "st,sd->td", dispatch, returned, preferred_element_type=jnp.float32
    ).astype(jnp.bfloat16)
    grad_shard = lax.psum_scatter(
        jnp.einsum("sxcd,sxcf->dxf", rows_in, hidden_grad, preferred_element_type=jnp.float32),
        "dp",
        scatter_dimension=0,
        tiled=True,
    )
    grad_scale = 1.0 / math.sqrt(tok_rows * n_expert * n_data)
    grad_shard = jnp.transpose(grad_shard * grad_scale, (1, 0, 2))
    return (token_grad, grad_shard[:, :, :hidden], grad_shard[:, :, hidden:])


def solution(mesh):
    placed = (
        P(("expert", "dp"), None),
        P(("expert", "dp"), None),
        P(("expert", "dp"), None),
        P(("expert", "dp"), None),
        P("expert", "dp", None),
        P("expert", "dp", None),
        P("expert", "dp", None),
    )
    return jax.shard_map(
        local,
        mesh=mesh,
        in_specs=placed,
        out_specs=(P(("expert", "dp"), None), P("expert", "dp", None), P("expert", "dp", None)),
        check_vma=False,
    )
```

profile of v0, /device:TPU:0, one launch (start us, length us, event | category | flops | bytes accessed | tf_op | source)
XLA Modules:
  0.0 414.8 jit_solution(15491095385532361212)
XLA Ops:
  8.0 0.7 all-gather.4.cloned.1.call-update
  9.4 0.8 copy.49
  11.6 0.7 multiply_add_fusion
  13.0 2.0 convolution_convert_fusion
  15.0 4.2 %all-to-all-start.1 = ((bf16[2,160,3072]{2,1,0:T(8,128)(2,1)}), bf16[2,160,3072]{2,1,0:T(8,128)(2,1)S(1)}, u32[]{:S(2)}, u32[]{:S(2)}) async-start(bf16[2,160,3072]{2,1,0:T(8,128)(2,1)} %bitcast.58), calls=%async_computation.1 | async-start | bytes 3932160 | tf_op jit(solution)/shard_map/all_to_all | solution.py:41
  19.4 2.8 fusion.3
  22.1 21.5 %all-to-all-done.1 = bf16[2,160,3072]{2,1,0:T(8,128)(2,1)S(1)} async-done(((bf16[2,160,3072]{2,1,0:T(8,128)(2,1)}), bf16[2,160,3072]{2,1,0:T(8,128)(2,1)S(1)}, u32[]{:S(2)}, u32[]{:S(2)}) %all-to-all-start.1) | async-done | bytes 1966112 | tf_op jit(solution)/shard_map/all_to_all | solution.py:41
  43.6 4.8 %all-to-all-start = ((bf16[2,160,3072]{2,1,0:T(8,128)(2,1)}), bf16[2,160,3072]{2,1,0:T(8,128)(2,1)}, u32[]{:S(2)}, u32[]{:S(2)}) async-start(bf16[2,160,3072]{2,1,0:T(8,128)(2,1)} %bitcast.56), calls=%async_computation | async-start | bytes 3932160 | tf_op jit(solution)/shard_map/all_to_all | solution.py:42
  48.5 9.9 %all-gather.6.cloned.1.call-done = bf16[4,3072,128]{2,1,0:T(8,128)(2,1)} async-done(((bf16[4,192,128]{2,1,0:T(8,128)(2,1)}), bf16[4,3072,128]{2,1,0:T(8,128)(2,1)}) %all-gather.6.cloned.1.call-update) | async-done | bytes 3145744 | tf_op jit(solution)/shard_map/all_gather | solution.py:37
  58.4 46.0 %all-gather.4.cloned.1.call-done = bf16[4,3072,128]{2,1,0:T(8,128)(2,1)} async-done(((bf16[4,192,128]{2,1,0:T(8,128)(2,1)}), bf16[4,3072,128]{2,1,0:T(8,128)(2,1)}) %all-gather.4.cloned.1.call-update) | async-done | bytes 3145744 | tf_op jit(solution)/shard_map/all_gather | solution.py:36
  104.4 3.5 fusion.10
  107.9 42.6 %all-gather.8.cloned.1.call-done = bf16[4,3072,128]{2,1,0:T(8,128)(2,1)} async-done(((bf16[4,192,128]{2,1,0:T(8,128)(2,1)}), bf16[4,3072,128]{2,1,0:T(8,128)(2,1)}) %all-gather.8.cloned.1.call-update) | async-done | bytes 3145744 | tf_op jit(solution)/shard_map/all_gather | solution.py:38
  150.5 3.3 fusion.22
  153.8 6.3 %convolution_bitcast_fusion = f32[3072,4,256]{0,2,1:T(8,128)} fusion(bf16[2,4,40,3072]{3,2,1,0:T(8,128)(2,1)S(1)} %bitcast.54, bf16[2,4,40,128]{3,2,0,1:T(8,128)(2,1)S(1)} %get-tuple-element.21, bf16[2,4,40,128]{3,2,0,1:T(8,128)(2,1)S(1)} %get-tuple-element.20), kind=kOutput, calls=%fused_computation | convolution fusion | flops 503644160 | bytes 14712832 | tf_op jit(solution)/shard_map/sxcd,sxcf->dxf/dot_general | solution.py:71
  160.1 14.6 %copy.56 = f32[3072,4,256]{2,1,0:T(4,128)} copy(f32[3072,4,256]{0,2,1:T(8,128)} %convolution_bitcast_fusion) | data formatting | bytes 25165824 | tf_op jit(solution)/shard_map/sxcd,sxcf->dxf/transpose | solution.py:71
  174.7 4.9 %fusion.4 = bf16[2,4,40,3072]{3,2,0,1:T(8,128)(2,1)S(1)} fusion(bf16[4,3072,128]{2,1,0:T(8,128)(2,1)} %all-gather.6.cloned.1.call-done, bf16[4,3072,128]{2,1,0:T(8,128)(2,1)} %all-gather.4.cloned.1.call-done, bf16[2,4,40,128]{3,2,0,1:T(8,128)(2,1)S(1)} %get-tuple-element.21, bf16[2,4,40,128]{3,2,0,1:T(8,128)(2,1)S(1)} %get-tuple-element.20), kind=kOutput, calls=%fused_computation.8 | convolution fusion | flops 517210112 | bytes 8421376 | tf_op jit(solution)/shard_map/sxcf,xdf->sxcd/dot_general | solution.py:56
  179.6 1.5 copy.54
  181.1 3.8 all-to-all-start.2
  186.1 22.8 %all-to-all-done.2 = bf16[2,160,3072]{2,1,0:T(8,128)(2,1)S(1)} async-done(((bf16[2,160,3072]{2,1,0:T(8,128)(2,1)}), bf16[2,160,3072]{2,1,0:T(8,128)(2,1)S(1)}, u32[]{:S(2)}, u32[]{:S(2)}) %all-to-all-start.2) | async-done | bytes 1966112 | tf_op jit(solution)/shard_map/all_to_all | solution.py:59
  208.9 1.5 convolution_convert_fusion.1
  210.4 194.9 %all-reduce.3.cloned.1.call-done = f32[3072,4,256]{2,1,0:T(4,128)} async-done(((f32[3072,4,256]{2,1,0:T(4,128)}), f32[3072,4,256]{2,1,0:T(4,128)}) %all-reduce.3.cloned.1.call-update) | async-done | bytes 12582928
  405.3 1.3 fusion.18
  406.8 0.8 copy.57
  407.5 0.8 copy.58
  (34 shorter events, 4.5 us)
Async XLA Ops:
  7.2 5.8 %copy-start = (bf16[128,3072]{1,0:T(8,128)(2,1)S(1)}, bf16[128,3072]{1,0:T(8,128)(2,1)}, u32[]{:S(2)}) copy-start(bf16[128,3072]{1,0:T(8,128)(2,1)} %param.7) | copy-start | bytes 2359300
  7.2 51.2 %all-gather.6.cloned.1.call-start = ((), (), s32[]{:S(2)}) async-start(), calls=%async_computation.4 | async-start | bytes 3342336 | tf_op jit(solution)/shard_map/all_gather | solution.py:37
  7.9 96.5 %all-gather.4.cloned.1.call-start = ((), (), s32[]{:S(2)}) async-start(), calls=%async_computation.3 | async-start | bytes 3342336 | tf_op jit(solution)/shard_map/all_gather | solution.py:36
  8.7 141.8 %all-gather.8.cloned.1.call-start = ((), (), s32[]{:S(2)}) async-start(), calls=%async_computation.5 | async-start | bytes 3342336 | tf_op jit(solution)/shard_map/all_gather | solution.py:38
  12.4 0.6 copy-start.2
  13.0 6.2 %copy-start.4 = (f32[128,2]{0,1:T(2,128)S(1)}, f32[128,2]{0,1:T(2,128)}, u32[]{:S(2)}) copy-start(f32[128,2]{0,1:T(2,128)} %param.10) | copy-start | bytes 3076
  13.0 6.4 %copy-start.1 = (bf16[128,3072]{1,0:T(8,128)(2,1)S(1)}, bf16[128,3072]{1,0:T(8,128)(2,1)}, u32[]{:S(2)}) copy-start(bf16[128,3072]{1,0:T(8,128)(2,1)} %param.8) | copy-start | bytes 2359300
  15.0 28.7 %all-to-all-start.1 = ((bf16[2,160,3072]{2,1,0:T(8,128)(2,1)}), bf16[2,160,3072]{2,1,0:T(8,128)(2,1)S(1)}, u32[]{:S(2)}, u32[]{:S(2)}) async-start(bf16[2,160,3072]{2,1,0:T(8,128)(2,1)} %bitcast.58), calls=%async_computation.1 | async-start | bytes 3932160 | tf_op jit(solution)/shard_map/all_to_all | solution.py:41
  43.6 64.2 %all-to-all-start = ((bf16[2,160,3072]{2,1,0:T(8,128)(2,1)}), bf16[2,160,3072]{2,1,0:T(8,128)(2,1)}, u32[]{:S(2)}, u32[]{:S(2)}) async-start(bf16[2,160,3072]{2,1,0:T(8,128)(2,1)} %bitcast.56), calls=%async_computation | async-start | bytes 3932160 | tf_op jit(solution)/shard_map/all_to_all | solution.py:42
  48.4 356.9 %all-reduce.3.cloned.1.call-start = ((), (), s32[]{:S(2)}) async-start(), calls=%async_computation.6 | async-start | bytes 25165824
  179.6 5.3 %copy-start.5 = (u32[32]{0:T(128)S(1)}, u32[32]{0:T(128)}, u32[]{:S(2)}) copy-start(u32[32]{0:T(128)} %constant.21) | copy-start | bytes 388
  179.6 29.3 %copy-start.3 = (pred[320,128]{1,0:T(8,128)(4,1)S(1)}, pred[320,128]{1,0:T(8,128)(4,1)}, u32[]{:S(2)}) copy-start(pred[320,128]{1,0:T(8,128)(4,1)} %copy-done.2) | copy-start | bytes 122884
  181.1 27.9 %all-to-all-start.2 = ((bf16[2,160,3072]{2,1,0:T(8,128)(2,1)}), bf16[2,160,3072]{2,1,0:T(8,128)(2,1)S(1)}, u32[]{:S(2)}, u32[]{:S(2)}) async-start(bf16[2,160,3072]{2,1,0:T(8,128)(2,1)} %bitcast.57), calls=%async_computation.2 | async-start | bytes 3932160 | tf_op jit(solution)/shard_map/all_to_all | solution.py:59
Sparse Core Ops, SparseCore 0:
  10.3 48.0 all-gather.5
  60.7 43.6 all-gather.3
  106.7 43.7 all-gather.7
  174.8 230.4 all-reduce.2
where the time goes:
time: 416 us; the launch traced here: 415 us
  waiting for transfers between devices  340 us (82%)
  matrix products  24.2 us (6%)
  local copies, waits for them, and re-layouts  20.4 us (5%)
  between operations  14.6 us (4%)
  starting transfers between devices  12.9 us (3%)
    unnamed x5, waiting for transfers between devices  197 us
    all_gather x1, waiting for transfers between devices, local(): lax.all_gather(w_gate, 'dp', axis=1, tiled=True)  46 us
    all_gather x1, waiting for transfers between devices, local(): lax.all_gather(w_down_t, 'dp', axis=1, tiled=True)  42.6 us
    all_to_all x1, waiting for transfers between devices, local(): lax.all_to_all(slot_input.reshape(n_expert, local_count * CAP, model_widt...  22.8 us
    all_to_all x1, waiting for transfers between devices, local(): lax.all_to_all(rows_out, 'expert', split_axis=0, concat_axis=0, tiled=True)  21.5 us
    transpose x1, local copies, waits for them, and re-layouts, local(): jnp.einsum('sxcd,sxcf->dxf', rows_in, hidden_grad, preferred_element_type...  14.6 us
    all_gather x1, waiting for transfers between devices, local(): lax.all_gather(w_up, 'dp', axis=1, tiled=True)  9.91 us
  transfers between devices with their start and end apart: 7, of which 6 were waited for; matrix products, arithmetic and copies ran while one was open for 5% of the time, Pallas kernels for 0%

commit v1 on v0

v1 whole, which is shorter than its diff:
```python
import functools
import math

import jax
import jax.numpy as jnp
from jax import lax
from jax.experimental import pallas as pl
from jax.experimental.pallas import tpu as pltpu
from jax.sharding import PartitionSpec as P

EXPERTS = 8
CAP = 40
INFO = 16
F32 = jnp.float32
BF16 = jnp.bfloat16


def remote(src, dst, send, recv, e, d):
    return pltpu.make_async_remote_copy(
        src_ref=src,
        dst_ref=dst,
        send_sem=send,
        recv_sem=recv,
        device_id={"expert": e, "dp": d},
        device_id_type=pl.DeviceIdType.MESH,
    )


def when(cond, fn):
    if cond is None:
        fn()
    else:
        pl.when(cond)(fn)


class Sends:
    def __init__(self):
        self.items = []

    def start(self, cond, make):
        when(cond, lambda: make().start())
        self.items.append((cond, make))

    def finish(self):
        for cond, make in self.items:
            when(cond, lambda make=make: make().wait_send())


def barrier(e, d, n_expert, n_data):
    sem = pltpu.get_barrier_semaphore()
    for j in range(1, n_data):
        pl.semaphore_signal(
            sem,
            inc=1,
            device_id={"expert": e, "dp": lax.rem(d + j, n_data)},
            device_id_type=pl.DeviceIdType.MESH,
        )
    for j in range(1, n_expert):
        pl.semaphore_signal(
            sem,
            inc=1,
            device_id={"expert": lax.rem(e + j, n_expert), "dp": d},
            device_id_type=pl.DeviceIdType.MESH,
        )
    pl.semaphore_wait(sem, n_data - 1 + n_expert - 1)


def both(p, q):
    if p is None:
        return q
    return jnp.logical_and(p, q)


def gather(e, d, n_data, owns, block, sems, sends, midway=None):
    up_s, down_s, b_s, c_s, recv = sems
    count = n_data // 4
    a, b, c = d // 4, lax.rem(d // 2, 2), lax.rem(d, 2)
    number = len(owns)

    def index(a2, b2, c2):
        return (a2 * 2 + b2) * 2 + c2

    def make(i, src, d2, target, send):
        return remote(src, block(i, d2), send, recv.at[i, d2], e, target)

    def arrive(i, d2):
        remote(block(i, d2), block(i, d2), c_s.at[i, 0], recv.at[i, d2], e, d).wait_recv()

    def pass_on(cond, i, src, a2, up, down, slot):
        d2 = index(a2, b, c)
        if up:
            sends.start(
                both(cond, a < count - 1),
                lambda: make(i, src(), d2, index(a + 1, b, c), up_s.at[i, slot]),
            )
        if down:
            sends.start(
                both(cond, a > 0),
                lambda: make(i, src(), d2, index(a - 1, b, c), down_s.at[i, slot]),
            )
        sends.start(cond, lambda: make(i, src(), d2, index(a, 1 - b, c), b_s.at[i, a2]))
        sends.start(cond, lambda: make(i, src(), d2, index(a, b, 1 - c), c_s.at[i, a2 * 2 + b]))

    def from_b(cond, a2):
        d2 = index(a2, 1 - b, c)
        for i in range(number):
            when(cond, lambda i=i: arrive(i, d2))
            sends.start(
                cond,
                lambda i=i: make(
                    i, block(i, d2), d2, index(a, b, 1 - c), c_s.at[i, a2 * 2 + 1 - b]
                ),
            )

    for i in range(number):
        pass_on(None, i, lambda i=i: owns[i], a, True, True, 0)
    if midway is not None:
        midway()
    for step in range(1, count):
        for i in range(number):
            cond, a2 = a >= step, a - step
            d2 = index(a2, b, c)
            when(cond, lambda i=i, d2=d2: arrive(i, d2))
            pass_on(cond, i, lambda i=i, d2=d2: block(i, d2), a2, True, False, step)
            cond, a2 = a + step < count, a + step
            d2 = index(a2, b, c)
            when(cond, lambda i=i, d2=d2: arrive(i, d2))
            pass_on(cond, i, lambda i=i, d2=d2: block(i, d2), a2, False, True, step)
        if step == 1:
            from_b(None, a)
        else:
            from_b(a >= step - 1, a - step + 1)
            from_b(a + step - 1 < count, a + step - 1)
    if count == 1:
        from_b(None, a)
    else:
        from_b(a >= count - 1, a - count + 1)
        from_b(a + count - 1 < count, a + count - 1)
    for a2 in range(count):
        for b2 in range(2):
            for i in range(number):
                arrive(i, index(a2, b2, 1 - c))


def first_kernel(
    n_expert, n_data, w_in, w_dn, tok, og, info, blocks,
    all_in, all_dn, tx, ox, ix, tt,
    own_sem, up_s, down_s, b_s, c_s, recv, x_s, x_r, t_s, t_r, y_s, y_r,
):
    e, d = lax.axis_index("expert"), lax.axis_index("dp")
    width = w_in.shape[1]
    rows = tok.shape[0]

    def block(i, d2):
        return (all_in, all_dn)[i].at[:, pl.ds(d2 * width, width), :]

    def columns(e2, d2):
        return tt.at[:, pl.ds(pl.multiple_of((e2 * n_data + d2) * rows, rows), rows)]

    def half(e2):
        return tt.at[:, pl.ds(pl.multiple_of(e2 * n_data * rows, n_data * rows), n_data * rows)]

    own = [
        pltpu.make_async_copy(w_in, block(0, d), own_sem.at[0]),
        pltpu.make_async_copy(w_dn, block(1, d), own_sem.at[1]),
        pltpu.make_async_copy(tok, tx.at[e], own_sem.at[2]),
        pltpu.make_async_copy(og, ox.at[e], own_sem.at[3]),
        pltpu.make_async_copy(info, ix.at[e], own_sem.at[4]),
        pltpu.make_async_copy(blocks.at[d], columns(e, d), own_sem.at[5]),
    ]
    for copy in own:
        copy.start()
    barrier(e, d, n_expert, n_data)
    sends = Sends()
    triples = ((tok, tx), (og, ox), (info, ix))

    def midway():
        for j in range(1, n_expert):
            for i, (src, dst) in enumerate(triples):
                sends.start(
                    None,
                    lambda i=i, j=j, src=src, dst=dst: remote(
                        src, dst.at[e], x_s.at[i, j], x_r.at[i, j], lax.rem(e + j, n_expert), d
                    ),
                )
        for j in range(1, n_data):
            sends.start(
                None,
                lambda j=j: remote(
                    blocks.at[lax.rem(d + j, n_data)], columns(e, d), t_s.at[j], t_r.at[j],
                    e, lax.rem(d + j, n_data),
                ),
            )

    gather(e, d, n_data, (w_in, w_dn), block, (up_s, down_s, b_s, c_s, recv), sends, midway)
    for copy in own:
        copy.wait()
    for j in range(1, n_data):
        source = lax.rem(d - j + n_data, n_data)
        remote(columns(e, source), columns(e, source), t_s.at[j], t_r.at[j], e, source).wait_recv()
    for j in range(1, n_expert):
        sends.start(
            None,
            lambda j=j: remote(half(e), half(e), y_s.at[j], y_r.at[j], lax.rem(e + j, n_expert), d),
        )
    for j in range(1, n_expert):
        source = lax.rem(e - j + n_expert, n_expert)
        for i, (src, dst) in enumerate(triples):
            remote(src, dst.at[source], x_s.at[i, j], x_r.at[i, j], source, d).wait_recv()
        remote(half(source), half(source), y_s.at[j], y_r.at[j], source, d).wait_recv()
    sends.finish()


def second_kernel(
    n_expert, n_data, hid, ret, all_hid, rx, own_sem, up_s, down_s, b_s, c_s, recv, x_s, x_r
):
    e, d = lax.axis_index("expert"), lax.axis_index("dp")

    def block(i, d2):
        return all_hid.at[d2]

    own = [
        pltpu.make_async_copy(hid, block(0, d), own_sem.at[0]),
        pltpu.make_async_copy(ret.at[e], rx.at[e], own_sem.at[1]),
    ]
    for copy in own:
        copy.start()
    barrier(e, d, n_expert, n_data)
    sends = Sends()

    def midway():
        for j in range(1, n_expert):
            target = lax.rem(e + j, n_expert)
            sends.start(
                None,
                lambda j=j, target=target: remote(
                    ret.at[target], rx.at[e], x_s.at[j], x_r.at[j], target, d
                ),
            )

    gather(e, d, n_data, (hid,), block, (up_s, down_s, b_s, c_s, recv), sends, midway)
    for copy in own:
        copy.wait()
    for j in range(1, n_expert):
        source = lax.rem(e - j + n_expert, n_expert)
        remote(ret.at[source], rx.at[source], x_s.at[j], x_r.at[j], source, d).wait_recv()
    sends.finish()


def picker(e0, p0, e1, p1, expert, n_expert, rows):
    shape = (n_expert * CAP, n_expert * rows)
    slot = lax.broadcasted_iota(jnp.int32, shape, 0)
    base = (lax.broadcasted_iota(jnp.int32, (1, shape[1]), 1) // rows) * CAP
    want0 = jnp.where(e0 == expert, p0.astype(jnp.int32) + base, -1)
    want1 = jnp.where(e1 == expert, p1.astype(jnp.int32) + base, -1)
    hit = jnp.logical_or(slot == want0, slot == want1)
    return jnp.where(hit, 1.0, 0.0).astype(BF16)


def compute_kernel(n_expert, tx, ox, info_r, info_c, w_in, w_dn, hid, ret, acc):
    x, local_count = pl.program_id(0), pl.num_programs(0)
    hidden = w_dn.shape[2]
    rows = tx.shape[0] // n_expert
    expert = (lax.axis_index("expert") * local_count + x).astype(F32)
    gate_up = jnp.dot(tx[...], w_in[0], preferred_element_type=F32)
    back = jnp.dot(ox[...], w_dn[0], preferred_element_type=F32)
    gate = jnp.where(info_c[:, 0:1] == expert, info_c[:, 4:5], 0.0) + jnp.where(
        info_c[:, 2:3] == expert, info_c[:, 5:6], 0.0
    )
    act_grad = back * gate
    gate_pre, up_pre = gate_up[:, :hidden], gate_up[:, hidden:]
    s = jax.nn.sigmoid(gate_pre)
    gate_grad = act_grad * up_pre * s * (1.0 + gate_pre * (1.0 - s))
    up_grad = act_grad * (gate_pre * s)
    grad = jnp.concatenate([gate_grad, up_grad], axis=1).astype(BF16)
    pick = picker(
        info_r[0:1, :], info_r[1:2, :], info_r[2:3, :], info_r[3:4, :], expert, n_expert, rows
    )
    hid[0] = jnp.dot(pick, grad, preferred_element_type=F32).astype(BF16)
    term = lax.dot_general(grad, w_in[0], (((1,), (1,)), ((), ())), preferred_element_type=F32)

    @pl.when(x == 0)
    def _():
        acc[...] = term

    @pl.when(x > 0)
    def _():
        acc[...] += term

    @pl.when(x == local_count - 1)
    def _():
        ret[...] = acc[...].astype(BF16)


def grad_kernel(n_expert, local_count, scale, *refs):
    tts, (hid, out_g, out_u) = refs[:n_expert], refs[n_expert:]
    step, steps = pl.program_id(0), pl.num_programs(0)
    width, hidden = out_g.shape[1], out_g.shape[2]
    rows = tts[0].shape[1]
    tok = jnp.concatenate([t[:width, :] for t in tts], axis=1)
    info = jnp.concatenate([t[width:, :] for t in tts], axis=1).astype(F32)

    @pl.when(step == 0)
    def _():
        out_g[...] = jnp.zeros_like(out_g)
        out_u[...] = jnp.zeros_like(out_u)

    for x in range(local_count):
        expert = (lax.axis_index("expert") * local_count + x).astype(F32)
        pick = picker(info[0:1], info[1:2], info[2:3], info[3:4], expert, n_expert, rows)
        got = lax.dot_general(
            tok, pick, (((1,), (1,)), ((), ())), preferred_element_type=F32
        ).astype(BF16)
        term = jnp.dot(got, hid[0, x], preferred_element_type=F32) * scale
        out_g[x] += term[:, :hidden]
        out_u[x] += term[:, hidden:]


def local(tokens, out_grad, routes, gates, w_gate, w_up, w_down_t):
    rows, model = tokens.shape
    n_expert = lax.axis_size("expert")
    n_data = lax.axis_size("dp")
    local_count, width, hidden = w_gate.shape
    count = n_data // 4
    any_, vmem = pl.BlockSpec(memory_space=pl.ANY), pl.BlockSpec(memory_space=pltpu.VMEM)
    dma = pltpu.SemaphoreType.DMA

    flat = routes.reshape(-1)
    onehot = (flat[:, None] == jnp.arange(EXPERTS, dtype=jnp.int32)[None, :]).astype(jnp.int32)
    position = jnp.sum((jnp.cumsum(onehot, axis=0) - 1) * onehot, axis=1).reshape(rows, 2)
    info = jnp.stack(
        [
            routes[:, 0].astype(F32), position[:, 0].astype(F32),
            routes[:, 1].astype(F32), position[:, 1].astype(F32),
            gates[:, 0], gates[:, 1], gates[:, 0], gates[:, 1],
        ]
    )
    side = jnp.concatenate([info[:4].astype(BF16), jnp.zeros((INFO - 4, rows), BF16)], axis=0)
    blocks = jnp.concatenate(
        [
            tokens.T.reshape(n_data, width, rows),
            jnp.broadcast_to(side[None], (n_data, INFO, rows)),
        ],
        axis=1,
    )
    w_in = jnp.concatenate([w_gate, w_up], axis=2)

    def chain_sems(number):
        return [
            dma((number, count)), dma((number, count)), dma((number, count)),
            dma((number, 2 * count)), dma((number, n_data)),
        ]

    shape = jax.ShapeDtypeStruct
    all_in, all_dn, tx, ox, ix, tt = pl.pallas_call(
        functools.partial(first_kernel, n_expert, n_data),
        out_shape=(
            shape((local_count, model, 2 * hidden), BF16),
            shape((local_count, model, hidden), BF16),
            shape((n_expert, rows, model), BF16),
            shape((n_expert, rows, model), BF16),
            shape((n_expert, 8, rows), F32),
            shape((width + INFO, n_expert * n_data * rows), BF16),
        ),
        in_specs=[vmem] * 6,
        out_specs=[any_] * 6,
        scratch_shapes=[dma((6,))]
        + chain_sems(2)
        + [
            dma((3, n_expert)), dma((3, n_expert)), dma((n_data,)), dma((n_data,)),
            dma((n_expert,)), dma((n_expert,)),
        ],
        compiler_params=pltpu.CompilerParams(collective_id=0, has_side_effects=True),
    )(w_in, w_down_t, tokens, out_grad, info, blocks)

    info_r = jnp.transpose(ix, (1, 0, 2)).reshape(8, n_expert * rows)
    info_c = info_r.T
    total = n_expert * rows
    slots = n_expert * CAP
    hid, ret = pl.pallas_call(
        functools.partial(compute_kernel, n_expert),
        grid=(local_count,),
        out_shape=(shape((local_count, slots, 2 * hidden), BF16), shape((total, model), BF16)),
        in_specs=[
            pl.BlockSpec((total, model), lambda x: (0, 0)),
            pl.BlockSpec((total, model), lambda x: (0, 0)),
            pl.BlockSpec((8, total), lambda x: (0, 0)),
            pl.BlockSpec((total, 8), lambda x: (0, 0)),
            pl.BlockSpec((1, model, 2 * hidden), lambda x: (x, 0, 0)),
            pl.BlockSpec((1, model, hidden), lambda x: (x, 0, 0)),
        ],
        out_specs=[
            pl.BlockSpec((1, slots, 2 * hidden), lambda x: (x, 0, 0)),
            pl.BlockSpec((total, model), lambda x: (0, 0)),
        ],
        scratch_shapes=[pltpu.VMEM((total, model), F32)],
        compiler_params=pltpu.CompilerParams(vmem_limit_bytes=60 * 1024 * 1024),
    )(tx.reshape(total, model), ox.reshape(total, model), info_r, info_c, all_in, all_dn)

    all_hid, rx = pl.pallas_call(
        functools.partial(second_kernel, n_expert, n_data),
        out_shape=(
            shape((n_data, local_count, slots, 2 * hidden), BF16),
            shape((n_expert, rows, model), BF16),
        ),
        in_specs=[vmem] * 2,
        out_specs=[any_] * 2,
        scratch_shapes=[dma((2,))] + chain_sems(1) + [dma((n_expert,)), dma((n_expert,))],
        compiler_params=pltpu.CompilerParams(collective_id=1, has_side_effects=True),
    )(hid, ret.reshape(n_expert, rows, model))

    token_grad = jnp.sum(rx.astype(F32), axis=0).astype(BF16)
    grad_scale = 1.0 / math.sqrt(rows * n_expert * n_data)

    def tt_spec(s):
        return pl.BlockSpec((width + INFO, rows), lambda i: (0, s * n_data + i))

    grad_gate, grad_up = pl.pallas_call(
        functools.partial(grad_kernel, n_expert, local_count, grad_scale),
        grid=(n_data,),
        out_shape=(
            shape((local_count, width, hidden), F32),
            shape((local_count, width, hidden), F32),
        ),
        in_specs=[tt_spec(s) for s in range(n_expert)]
        + [pl.BlockSpec((1, local_count, slots, 2 * hidden), lambda i: (i, 0, 0, 0))],
        out_specs=[pl.BlockSpec((local_count, width, hidden), lambda i: (0, 0, 0))] * 2,
    )(*([tt] * n_expert), all_hid)
    return token_grad, grad_gate, grad_up


def solution(mesh):
    row, split = P(("expert", "dp"), None), P("expert", "dp", None)
    return jax.shard_map(
        local,
        mesh=mesh,
        in_specs=(row, row, row, row, split, split, split),
        out_specs=(row, split, split),
        check_vma=False,
    )
```

time: 416 us -> 157 us (0.38)
  waiting for transfers between devices: 340 us -> 0 us
  Pallas kernels: 0 us -> 145 us
  matrix products: 24.2 us -> 0 us
  local copies, waits for them, and re-layouts: 20.4 us -> 4.69 us
  between operations: 14.6 us -> 0.73 us
  starting transfers between devices: 12.9 us -> 0 us
    unnamed x5 -> x0, waiting for transfers between devices: 197 us -> none
    pallas_call x0 -> x4, Pallas kernels: none -> 145 us  [the longest x1 93.2 us: local(): pl.pallas_call(functools.partial(first_kernel, n_expert, n_data), out_sha...]
    all_gather x3 -> x0, waiting for transfers between devices: 98.5 us -> none  [the longest x1 46 us: local(): lax.all_gather(w_gate, 'dp', axis=1, tiled=True)]
    all_to_all x3 -> x0, waiting for transfers between devices: 44.4 us -> none  [the longest x1 22.8 us: local(): lax.all_to_all(slot_input.reshape(n_expert, local_count * CAP, model_widt...]
    dot_general x7 -> x0, matrix products: 24.2 us -> none  [the longest x1 6.3 us: local(): jnp.einsum('sxcd,sxcf->dxf', rows_in, hidden_grad, preferred_element_type...]
    transpose x1 -> x2, local copies, waits for them, and re-layouts: 14.6 us -> 1.19 us  [the longest x1 0.82 us: local(): info_r = jnp.transpose(ix, (1, 0, 2)).reshape(8, n_expert * rows)]
    all_to_all x3 -> x0, starting transfers between devices: 12.8 us -> none  [the longest x1 4.76 us: local(): lax.all_to_all(grads_out, 'expert', split_axis=0, concat_axis=0, tiled=True)]
  transfers between devices with their start and end apart: 7 -> 0, of which waited for: 6 -> 0; matrix products, arithmetic and copies ran while one was open for 5% -> 0% of each run, Pallas kernels for 0% -> 0%
where the time goes in v1:
time: 157 us
  Pallas kernels  145 us (92%)
  other arithmetic  5.85 us (4%)
  local copies, waits for them, and re-layouts  4.69 us (3%)
    pallas_call x1, Pallas kernels, local(): pl.pallas_call(functools.partial(first_kernel, n_expert, n_data), out_sha...  93.2 us
    pallas_call x1, Pallas kernels, local(): pl.pallas_call(functools.partial(second_kernel, n_expert, n_data), out_sh...  26.2 us
    pallas_call x1, Pallas kernels, local(): pl.pallas_call(functools.partial(grad_kernel, n_expert, local_count, grad...  14.6 us
    pallas_call x1, Pallas kernels, local(): pl.pallas_call(functools.partial(compute_kernel, n_expert), grid=(local_c...  11.5 us

profile of v1, /device:TPU:0, one launch (start us, length us, event | category | flops | bytes accessed | tf_op | source)
XLA Modules:
  0.0 156.8 jit_solution(12438234376821105531)
XLA Ops:
  0.6 0.0 copy-start
  0.6 0.8 slice_bitcast_fusion
  1.4 0.8 fusion.11
  2.2 0.8 copy.18
  3.0 0.1 eq.29
  3.1 0.1 eq.25
  3.3 0.6 reduce-window.6
  3.8 0.2 slice_reduce_fusion
  4.1 0.1 fusion.6
  4.2 0.1 reshape.89
  4.3 0.2 fusion
  4.5 0.6 stack.4.info
  5.2 1.8 %pad_maximum_fusion.1.w_in = bf16[4,192,256]{2,1,0:T(8,128)(2,1)} fusion(bf16[4,192,128]{2,1,0:T(8,128)(2,1)} %param.12, bf16[4,192,128]{2,1,0:T(8,128)(2,1)} %param.11), kind=kLoop, calls=%fused_computation.1 | loop fusion | flops 786432 | bytes 786432 | tf_op jit(solution)/shard_map/concatenate | solution.py:346
  7.0 0.0 copy-done
  7.0 0.4 copy.20
  7.4 1.0 pad_maximum_fusion.blocks
  8.4 93.2 %shard_map.94 = (bf16[4,3072,256]{2,1,0:T(8,128)(2,1)}, bf16[4,3072,128]{2,1,0:T(8,128)(2,1)}, bf16[2,128,3072]{2,1,0:T(8,128)(2,1)}, bf16[2,128,3072]{2,1,0:T(8...) custom-call(bf16[4,192,256]{2,1,0:T(8,128)(2,1)} %pad_maximum_fusion.1.w_in, bf16[4,192,128]{2,1,0:T(8,128)(2,1)} %w_dn.1, ...), custom_call_target="tpu_custom_call" | custom-call | tf_op jit(solution)/shard_map/pallas_call | solution.py:355
  101.6 0.8 copy.21
  102.4 0.0 copy-start.2
  102.4 0.7 copy.22.info_r
  103.1 11.5 %shard_map.95 = (bf16[4,80,256]{2,1,0:T(8,128)(2,1)}, bf16[256,3072]{1,0:T(8,128)(2,1)}) custom-call(bf16[256,3072]{1,0:T(8,128)(2,1)} %bitcast.34, bf16[256,3072]{1,0:T(8,128)(2,1)} %bitcast.35, f32[8,256]{1,0:T(8,128)} %copy.22.info_r, f32[256,8]{1,0:T(8,128)} %bitcast.37, bf16[4,3072,256]{2,1,0:T(8,128)(2,1)} %get-tuple-element.18.w_in, ...), custom_call_target="tpu_custom_call" | custom-call | tf_op jit(solution)/shard_map/pallas_call | solution.py:380
  114.6 26.2 %shard_map.96 = (bf16[16,4,80,256]{3,2,1,0:T(8,128)(2,1)}, bf16[2,128,3072]{2,1,0:T(8,128)(2,1)}) custom-call(bf16[4,80,256]{2,1,0:T(8,128)(2,1)} %get-tuple-element.20.hid, bf16[2,128,3072]{2,1,0:T(8,128)(2,1)} %bitcast.33), custom_call_target="tpu_custom_call" | custom-call | tf_op jit(solution)/shard_map/pallas_call | solution.py:400
  140.8 14.6 %shard_map.97 = (f32[4,192,128]{2,1,0:T(8,128)}, f32[4,192,128]{2,1,0:T(8,128)}) custom-call(bf16[208,4096]{1,0:T(8,128)(2,1)} %get-tuple-element.23.refs_0_.refs_1_, bf16[208,4096]{1,0:T(8,128)(2,1)} %get-tuple-element.23.refs_0_.refs_1_, bf16[16,4,80,256]{3,2,1,0:T(8,128)(2,1)} %get-tuple-element.24.refs_2_), custom_call_target="tpu_custom_call" | custom-call | tf_op jit(solution)/shard_map/pallas_call | solution.py:418
  155.4 1.4 reduce_sum.22
  (9 shorter events, 0.1 us)
Async XLA Ops:
  0.6 6.4 %copy-start = (bf16[128,3072]{1,0:T(8,128)(2,1)S(1)}, bf16[128,3072]{1,0:T(8,128)(2,1)}, u32[]{:S(2)}) copy-start(bf16[128,3072]{1,0:T(8,128)(2,1)} %tok.1) | copy-start | bytes 2359300
  102.4 0.7 copy-start.2
  140.8 14.6 %copy-start.1 = (bf16[2,128,3072]{2,1,0:T(8,128)(2,1)S(1)}, bf16[2,128,3072]{2,1,0:T(8,128)(2,1)}, u32[]{:S(2)}) copy-start(bf16[2,128,3072]{2,1,0:T(8,128)(2,1)} %get-tuple-element.22) | copy-start | bytes 4718596

commit v2 on v1

--- a/solution.py
+++ b/solution.py
@@ -71,7 +71,7 @@
     return jnp.logical_and(p, q)
 
 
-def gather(e, d, n_data, owns, block, sems, sends, midway=None):
+def gather(e, d, n_data, owns, block, sems, sends, hook=None, use=None):
     up_s, down_s, b_s, c_s, recv = sems
     count = n_data // 4
     a, b, c = d // 4, lax.rem(d // 2, 2), lax.rem(d, 2)
@@ -112,34 +112,46 @@
                 ),
             )
 
-    for i in range(number):
-        pass_on(None, i, lambda i=i: owns[i], a, True, True, 0)
-    if midway is not None:
-        midway()
-    for step in range(1, count):
-        for i in range(number):
-            cond, a2 = a >= step, a - step
-            d2 = index(a2, b, c)
-            when(cond, lambda i=i, d2=d2: arrive(i, d2))
-            pass_on(cond, i, lambda i=i, d2=d2: block(i, d2), a2, True, False, step)
-            cond, a2 = a + step < count, a + step
-            d2 = index(a2, b, c)
-            when(cond, lambda i=i, d2=d2: arrive(i, d2))
-            pass_on(cond, i, lambda i=i, d2=d2: block(i, d2), a2, False, True, step)
+    for step in range(count + 2):
+        if step == 0:
+            for i in range(number):
+                pass_on(None, i, lambda i=i: owns[i], a, True, True, 0)
+        elif step < count:
+            for i in range(number):
+                cond, a2 = a >= step, a - step
+                d2 = index(a2, b, c)
+                when(cond, lambda i=i, d2=d2: arrive(i, d2))
+                pass_on(cond, i, lambda i=i, d2=d2: block(i, d2), a2, True, False, step)
+                cond, a2 = a + step < count, a + step
+                d2 = index(a2, b, c)
+                when(cond, lambda i=i, d2=d2: arrive(i, d2))
+                pass_on(cond, i, lambda i=i, d2=d2: block(i, d2), a2, False, True, step)
         if step == 1:
             from_b(None, a)
-        else:
+        elif 1 < step <= count:
             from_b(a >= step - 1, a - step + 1)
             from_b(a + step - 1 < count, a + step - 1)
-    if count == 1:
-        from_b(None, a)
-    else:
-        from_b(a >= count - 1, a - count + 1)
-        from_b(a + count - 1 < count, a + count - 1)
-    for a2 in range(count):
-        for b2 in range(2):
-            for i in range(number):
-                arrive(i, index(a2, b2, 1 - c))
+        if hook is not None:
+            hook(step, count)
+
+        def job(j, carry, step=step):
+            flip_b, flip_c, way = lax.rem(j // 2, 2), j // 4, lax.rem(j, 2)
+            shift = step - flip_b - flip_c
+            a2 = a - shift + 2 * shift * way
+            d2 = index(a2, b + flip_b * (1 - 2 * b), c + flip_c * (1 - 2 * c))
+            far = jnp.logical_or(shift > 0, jnp.logical_and(shift == 0, way == 0))
+            valid = jnp.logical_and(far, jnp.logical_and(a2 >= 0, a2 < count))
+
+            @pl.when(jnp.logical_and(valid, flip_c == 1))
+            def _():
+                for i in range(number):
+                    arrive(i, d2)
+
+            if use is not None:
+                pl.when(valid)(lambda: use(d2))
+            return carry
+
+        lax.fori_loop(0, 8, job, 0)
 
 
 def first_kernel(
@@ -174,7 +186,11 @@
     sends = Sends()
     triples = ((tok, tx), (og, ox), (info, ix))
 
-    def midway():
+    def hook(step, count):
+        if step == count - 1:
+            relay()
+        if step > 0:
+            return
         for j in range(1, n_expert):
             for i, (src, dst) in enumerate(triples):
                 sends.start(
@@ -192,17 +208,23 @@
                 ),
             )
 
-    gather(e, d, n_data, (w_in, w_dn), block, (up_s, down_s, b_s, c_s, recv), sends, midway)
-    for copy in own:
+    def relay():
+        own[5].wait()
+        for j in range(1, n_data):
+            source = lax.rem(d - j + n_data, n_data)
+            place = columns(e, source)
+            remote(place, place, t_s.at[j], t_r.at[j], e, source).wait_recv()
+        for j in range(1, n_expert):
+            sends.start(
+                None,
+                lambda j=j: remote(
+                    half(e), half(e), y_s.at[j], y_r.at[j], lax.rem(e + j, n_expert), d
+                ),
+            )
+
+    gather(e, d, n_data, (w_in, w_dn), block, (up_s, down_s, b_s, c_s, recv), sends, hook)
+    for copy in own[:5]:
         copy.wait()
-    for j in range(1, n_data):
-        source = lax.rem(d - j + n_data, n_data)
-        remote(columns(e, source), columns(e, source), t_s.at[j], t_r.at[j], e, source).wait_recv()
-    for j in range(1, n_expert):
-        sends.start(
-            None,
-            lambda j=j: remote(half(e), half(e), y_s.at[j], y_r.at[j], lax.rem(e + j, n_expert), d),
-        )
     for j in range(1, n_expert):
         source = lax.rem(e - j + n_expert, n_expert)
         for i, (src, dst) in enumerate(triples):
@@ -212,9 +234,12 @@
 
 
 def second_kernel(
-    n_expert, n_data, hid, ret, all_hid, rx, own_sem, up_s, down_s, b_s, c_s, recv, x_s, x_r
+    n_expert, n_data, scale, hid, ret, tt, rx, out_g, out_u,
+    all_hid, own_sem, up_s, down_s, b_s, c_s, recv, x_s, x_r,
 ):
     e, d = lax.axis_index("expert"), lax.axis_index("dp")
+    local_count, width, hidden = out_g.shape
+    rows = tt.shape[1] // (n_expert * n_data)
 
     def block(i, d2):
         return all_hid.at[d2]
@@ -228,7 +253,9 @@
     barrier(e, d, n_expert, n_data)
     sends = Sends()
 
-    def midway():
+    def hook(step, count):
+        if step > 0:
+            return
         for j in range(1, n_expert):
             target = lax.rem(e + j, n_expert)
             sends.start(
@@ -237,10 +264,29 @@
                     ret.at[target], rx.at[e], x_s.at[j], x_r.at[j], target, d
                 ),
             )
-
-    gather(e, d, n_data, (hid,), block, (up_s, down_s, b_s, c_s, recv), sends, midway)
-    for copy in own:
-        copy.wait()
+        out_g[...] = jnp.zeros_like(out_g)
+        out_u[...] = jnp.zeros_like(out_u)
+        own[0].wait()
+
+    def use(d2):
+        parts = [
+            tt[:, pl.ds(pl.multiple_of((s * n_data + d2) * rows, rows), rows)]
+            for s in range(n_expert)
+        ]
+        both_tt = jnp.concatenate(parts, axis=1)
+        tok, info = both_tt[:width], both_tt[width:].astype(F32)
+        for x in range(local_count):
+            expert = (e * local_count + x).astype(F32)
+            pick = picker(info[0:1], info[1:2], info[2:3], info[3:4], expert, n_expert, rows)
+            got = lax.dot_general(
+                tok, pick, (((1,), (1,)), ((), ())), preferred_element_type=F32
+            ).astype(BF16)
+            term = jnp.dot(got, all_hid[d2, x], preferred_element_type=F32) * scale
+            out_g[x] += term[:, :hidden]
+            out_u[x] += term[:, hidden:]
+
+    gather(e, d, n_data, (hid,), block, (up_s, down_s, b_s, c_s, recv), sends, hook, use)
+    own[1].wait()
     for j in range(1, n_expert):
         source = lax.rem(e - j + n_expert, n_expert)
         remote(ret.at[source], rx.at[source], x_s.at[j], x_r.at[j], source, d).wait_recv()
@@ -290,30 +336,6 @@
     @pl.when(x == local_count - 1)
     def _():
         ret[...] = acc[...].astype(BF16)
-
-
-def grad_kernel(n_expert, local_count, scale, *refs):
-    tts, (hid, out_g, out_u) = refs[:n_expert], refs[n_expert:]
-    step, steps = pl.program_id(0), pl.num_programs(0)
-    width, hidden = out_g.shape[1], out_g.shape[2]
-    rows = tts[0].shape[1]
-    tok = jnp.concatenate([t[:width, :] for t in tts], axis=1)
-    info = jnp.concatenate([t[width:, :] for t in tts], axis=1).astype(F32)
-
-    @pl.when(step == 0)
-    def _():
-        out_g[...] = jnp.zeros_like(out_g)
-        out_u[...] = jnp.zeros_like(out_u)
-
-    for x in range(local_count):
-        expert = (lax.axis_index("expert") * local_count + x).astype(F32)
-        pick = picker(info[0:1], info[1:2], info[2:3], info[3:4], expert, n_expert, rows)
-        got = lax.dot_general(
-            tok, pick, (((1,), (1,)), ((), ())), preferred_element_type=F32
-        ).astype(BF16)
-        term = jnp.dot(got, hid[0, x], preferred_element_type=F32) * scale
-        out_g[x] += term[:, :hidden]
-        out_u[x] += term[:, hidden:]
 
 
 def local(tokens, out_grad, routes, gates, w_gate, w_up, w_down_t):
@@ -397,35 +419,24 @@
         compiler_params=pltpu.CompilerParams(vmem_limit_bytes=60 * 1024 * 1024),
     )(tx.reshape(total, model), ox.reshape(total, model), info_r, info_c, all_in, all_dn)
 
-    all_hid, rx = pl.pallas_call(
-        functools.partial(second_kernel, n_expert, n_data),
+    grad_scale = 1.0 / math.sqrt(rows * n_expert * n_data)
+    rx, grad_gate, grad_up = pl.pallas_call(
+        functools.partial(second_kernel, n_expert, n_data, grad_scale),
         out_shape=(
-            shape((n_data, local_count, slots, 2 * hidden), BF16),
             shape((n_expert, rows, model), BF16),
-        ),
-        in_specs=[vmem] * 2,
-        out_specs=[any_] * 2,
-        scratch_shapes=[dma((2,))] + chain_sems(1) + [dma((n_expert,)), dma((n_expert,))],
-        compiler_params=pltpu.CompilerParams(collective_id=1, has_side_effects=True),
-    )(hid, ret.reshape(n_expert, rows, model))
-
-    token_grad = jnp.sum(rx.astype(F32), axis=0).astype(BF16)
-    grad_scale = 1.0 / math.sqrt(rows * n_expert * n_data)
-
-    def tt_spec(s):
-        return pl.BlockSpec((width + INFO, rows), lambda i: (0, s * n_data + i))
-
-    grad_gate, grad_up = pl.pallas_call(
-        functools.partial(grad_kernel, n_expert, local_count, grad_scale),
-        grid=(n_data,),
-        out_shape=(
             shape((local_count, width, hidden), F32),
             shape((local_count, width, hidden), F32),
         ),
-        in_specs=[tt_spec(s) for s in range(n_expert)]
-        + [pl.BlockSpec((1, local_count, slots, 2 * hidden), lambda i: (i, 0, 0, 0))],
-        out_specs=[pl.BlockSpec((local_count, width, hidden), lambda i: (0, 0, 0))] * 2,
-    )(*([tt] * n_expert), all_hid)
+        in_specs=[vmem] * 3,
+        out_specs=[any_, vmem, vmem],
+        scratch_shapes=[pltpu.VMEM((n_data, local_count, slots, 2 * hidden), BF16), dma((2,))]
+        + chain_sems(1)
+        + [dma((n_expert,)), dma((n_expert,))],
+        compiler_params=pltpu.CompilerParams(
+            collective_id=1, has_side_effects=True, vmem_limit_bytes=60 * 1024 * 1024
+        ),
+    )(hid, ret.reshape(n_expert, rows, model), tt)
+    token_grad = jnp.sum(rx.astype(F32), axis=0).astype(BF16)
     return token_grad, grad_gate, grad_up
 
 

time: 157 us -> 144 us (0.917)
  Pallas kernels: 145 us -> 130 us
    pallas_call x1, Pallas kernels: 93.2 us -> 83.4 us  [local(): pl.pallas_call(functools.partial(first_kernel, n_expert, n_data), out_sha...]
    pallas_call x2 -> x1, Pallas kernels: 40.8 us -> 34.7 us  [local(): pl.pallas_call(functools.partial(second_kernel, n_expert, n_data, grad_sc...]
where the time goes in v2:
time: 144 us
  Pallas kernels  130 us (90%)
  other arithmetic  7.33 us (5%)
  local copies, waits for them, and re-layouts  6.18 us (4%)
    pallas_call x1, Pallas kernels, local(): pl.pallas_call(functools.partial(first_kernel, n_expert, n_data), out_sha...  83.4 us
    pallas_call x1, Pallas kernels, local(): pl.pallas_call(functools.partial(second_kernel, n_expert, n_data, grad_sc...  34.7 us
    pallas_call x1, Pallas kernels, local(): pl.pallas_call(functools.partial(compute_kernel, n_expert), grid=(local_c...  11.5 us

profile of v2, /device:TPU:0, one launch (start us, length us, event | category | flops | bytes accessed | tf_op | source)
XLA Modules:
  0.0 143.8 jit_solution(6702437388633454832)
XLA Ops:
  0.6 0.0 copy-start
  0.6 0.8 slice_bitcast_fusion
  1.4 0.8 fusion.11
  2.2 0.8 copy.18
  3.0 0.1 eq.29
  3.1 0.1 eq.25
  3.3 0.6 reduce-window.6
  3.8 0.2 slice_reduce_fusion
  4.1 0.1 fusion.6
  4.2 0.1 reshape.89
  4.3 0.2 fusion
  4.5 0.6 stack.4.info
  5.2 1.8 %pad_maximum_fusion.1.w_in = bf16[4,192,256]{2,1,0:T(8,128)(2,1)} fusion(bf16[4,192,128]{2,1,0:T(8,128)(2,1)} %param.12, bf16[4,192,128]{2,1,0:T(8,128)(2,1)} %param.11), kind=kLoop, calls=%fused_computation.1 | loop fusion | flops 786432 | bytes 786432 | tf_op jit(solution)/shard_map/concatenate | solution.py:368
  7.0 0.4 copy.20
  7.4 1.0 pad_maximum_fusion.blocks
  8.3 83.4 %shard_map.94 = (bf16[4,3072,256]{2,1,0:T(8,128)(2,1)}, bf16[4,3072,128]{2,1,0:T(8,128)(2,1)}, bf16[2,128,3072]{2,1,0:T(8,128)(2,1)}, bf16[2,128,3072]{2,1,0:T(8...) custom-call(bf16[4,192,256]{2,1,0:T(8,128)(2,1)} %pad_maximum_fusion.1.w_in, bf16[4,192,128]{2,1,0:T(8,128)(2,1)} %w_dn.1, ...), custom_call_target="tpu_custom_call" | custom-call | tf_op jit(solution)/shard_map/pallas_call | solution.py:377
  91.8 0.8 copy.21
  92.6 0.0 copy-start.1
  92.6 0.7 copy.22.info_r
  93.3 11.5 %shard_map.95 = (bf16[4,80,256]{2,1,0:T(8,128)(2,1)}, bf16[256,3072]{1,0:T(8,128)(2,1)}) custom-call(bf16[256,3072]{1,0:T(8,128)(2,1)} %bitcast.34, bf16[256,3072]{1,0:T(8,128)(2,1)} %bitcast.35, f32[8,256]{1,0:T(8,128)} %copy.22.info_r, f32[256,8]{1,0:T(8,128)} %bitcast.37, bf16[4,3072,256]{2,1,0:T(8,128)(2,1)} %get-tuple-element.17.w_in, ...), custom_call_target="tpu_custom_call" | custom-call | tf_op jit(solution)/shard_map/pallas_call | solution.py:402
  104.7 34.7 %shard_map.96 = (bf16[2,128,3072]{2,1,0:T(8,128)(2,1)}, f32[4,192,128]{2,1,0:T(8,128)}, f32[4,192,128]{2,1,0:T(8,128)}) custom-call(bf16[4,80,256]{2,1,0:T(8,128)(2,1)} %get-tuple-element.19.hid, bf16[2,128,3072]{2,1,0:T(8,128)(2,1)} %bitcast.33, bf16[208,4096]{1,0:T(8,128)(2,1)} %get-tuple-element.21.tt), custom_call_target="tpu_custom_call" | custom-call | tf_op jit(solution)/shard_map/pallas_call | solution.py:423
  139.4 2.9 %reduce_sum.22 = bf16[128,3072]{1,0:T(8,128)(2,1)} reduce(bf16[2,128,3072]{2,1,0:T(8,128)(2,1)} %get-tuple-element.22, bf16[]{:T(256)} %constant.12.clone.1), dimensions={0}, to_apply=%region_3.4 | reduce | flops 393216 | bytes 2359298 | tf_op jit(solution)/shard_map/reduce_sum | solution.py:439
  142.3 0.7 copy.25
  143.0 0.7 copy.26
  (12 shorter events, 0.1 us)
Async XLA Ops:
  0.6 6.4 %copy-start = (bf16[128,3072]{1,0:T(8,128)(2,1)S(1)}, bf16[128,3072]{1,0:T(8,128)(2,1)}, u32[]{:S(2)}) copy-start(bf16[128,3072]{1,0:T(8,128)(2,1)} %tok.1) | copy-start | bytes 2359300
  92.6 0.7 copy-start.1
  139.4 2.9 %copy-start.3 = (f32[4,192,128]{2,1,0:T(8,128)S(1)}, f32[4,192,128]{2,1,0:T(8,128)}, u32[]{:S(2)}) copy-start(f32[4,192,128]{2,1,0:T(8,128)} %get-tuple-element.39) | copy-start | bytes 1179652
  139.4 3.6 %copy-start.2 = (f32[4,192,128]{2,1,0:T(8,128)S(1)}, f32[4,192,128]{2,1,0:T(8,128)}, u32[]{:S(2)}) copy-start(f32[4,192,128]{2,1,0:T(8,128)} %get-tuple-element.40) | copy-start | bytes 1179652

commit v3 on v2

--- a/solution.py
+++ b/solution.py
@@ -155,16 +155,16 @@
 
 
 def first_kernel(
-    n_expert, n_data, w_in, w_dn, tok, og, info, blocks,
-    all_in, all_dn, tx, ox, ix, tt,
+    n_expert, n_data, w_g, w_u, w_dn, tok, og, info, blocks,
+    all_g, all_u, all_dn, tx, ox, ix, tt,
     own_sem, up_s, down_s, b_s, c_s, recv, x_s, x_r, t_s, t_r, y_s, y_r,
 ):
     e, d = lax.axis_index("expert"), lax.axis_index("dp")
-    width = w_in.shape[1]
+    width = w_g.shape[1]
     rows = tok.shape[0]
 
     def block(i, d2):
-        return (all_in, all_dn)[i].at[:, pl.ds(d2 * width, width), :]
+        return (all_g, all_u, all_dn)[i].at[:, pl.ds(d2 * width, width), :]
 
     def columns(e2, d2):
         return tt.at[:, pl.ds(pl.multiple_of((e2 * n_data + d2) * rows, rows), rows)]
@@ -173,12 +173,13 @@
         return tt.at[:, pl.ds(pl.multiple_of(e2 * n_data * rows, n_data * rows), n_data * rows)]
 
     own = [
-        pltpu.make_async_copy(w_in, block(0, d), own_sem.at[0]),
-        pltpu.make_async_copy(w_dn, block(1, d), own_sem.at[1]),
+        pltpu.make_async_copy(w_g, block(0, d), own_sem.at[0]),
+        pltpu.make_async_copy(w_dn, block(2, d), own_sem.at[1]),
         pltpu.make_async_copy(tok, tx.at[e], own_sem.at[2]),
         pltpu.make_async_copy(og, ox.at[e], own_sem.at[3]),
         pltpu.make_async_copy(info, ix.at[e], own_sem.at[4]),
         pltpu.make_async_copy(blocks.at[d], columns(e, d), own_sem.at[5]),
+        pltpu.make_async_copy(w_u, block(1, d), own_sem.at[6]),
     ]
     for copy in own:
         copy.start()
@@ -187,10 +188,12 @@
     triples = ((tok, tx), (og, ox), (info, ix))
 
     def hook(step, count):
-        if step == count - 1:
+        if step == 0:
+            spread()
+        if step == max(count - 2, 0):
             relay()
-        if step > 0:
-            return
+
+    def spread():
         for j in range(1, n_expert):
             for i, (src, dst) in enumerate(triples):
                 sends.start(
@@ -222,8 +225,8 @@
                 ),
             )
 
-    gather(e, d, n_data, (w_in, w_dn), block, (up_s, down_s, b_s, c_s, recv), sends, hook)
-    for copy in own[:5]:
+    gather(e, d, n_data, (w_g, w_u, w_dn), block, (up_s, down_s, b_s, c_s, recv), sends, hook)
+    for copy in own[:5] + own[6:]:
         copy.wait()
     for j in range(1, n_expert):
         source = lax.rem(e - j + n_expert, n_expert)
@@ -234,8 +237,8 @@
 
 
 def second_kernel(
-    n_expert, n_data, scale, hid, ret, tt, rx, out_g, out_u,
-    all_hid, own_sem, up_s, down_s, b_s, c_s, recv, x_s, x_r,
+    n_expert, n_data, hid, ret, tt, tg, out_g, out_u,
+    all_hid, rx, own_sem, up_s, down_s, b_s, c_s, recv, x_s, x_r,
 ):
     e, d = lax.axis_index("expert"), lax.axis_index("dp")
     local_count, width, hidden = out_g.shape
@@ -244,12 +247,8 @@
     def block(i, d2):
         return all_hid.at[d2]
 
-    own = [
-        pltpu.make_async_copy(hid, block(0, d), own_sem.at[0]),
-        pltpu.make_async_copy(ret.at[e], rx.at[e], own_sem.at[1]),
-    ]
-    for copy in own:
-        copy.start()
+    own = pltpu.make_async_copy(hid, block(0, d), own_sem)
+    own.start()
     barrier(e, d, n_expert, n_data)
     sends = Sends()
 
@@ -266,7 +265,7 @@
             )
         out_g[...] = jnp.zeros_like(out_g)
         out_u[...] = jnp.zeros_like(out_u)
-        own[0].wait()
+        own.wait()
 
     def use(d2):
         parts = [
@@ -281,15 +280,17 @@
             got = lax.dot_general(
                 tok, pick, (((1,), (1,)), ((), ())), preferred_element_type=F32
             ).astype(BF16)
-            term = jnp.dot(got, all_hid[d2, x], preferred_element_type=F32) * scale
+            term = jnp.dot(got, all_hid[d2, x], preferred_element_type=F32)
             out_g[x] += term[:, :hidden]
             out_u[x] += term[:, hidden:]
 
     gather(e, d, n_data, (hid,), block, (up_s, down_s, b_s, c_s, recv), sends, hook, use)
-    own[1].wait()
+    total = ret[e].astype(F32)
     for j in range(1, n_expert):
         source = lax.rem(e - j + n_expert, n_expert)
         remote(ret.at[source], rx.at[source], x_s.at[j], x_r.at[j], source, d).wait_recv()
+        total += rx[source].astype(F32)
+    tg[...] = total.astype(BF16)
     sends.finish()
 
 
@@ -303,12 +304,15 @@
     return jnp.where(hit, 1.0, 0.0).astype(BF16)
 
 
-def compute_kernel(n_expert, tx, ox, info_r, info_c, w_in, w_dn, hid, ret, acc):
+def compute_kernel(n_expert, tx, ox, ix, w_g, w_u, w_dn, hid, ret, acc):
     x, local_count = pl.program_id(0), pl.num_programs(0)
     hidden = w_dn.shape[2]
     rows = tx.shape[0] // n_expert
     expert = (lax.axis_index("expert") * local_count + x).astype(F32)
-    gate_up = jnp.dot(tx[...], w_in[0], preferred_element_type=F32)
+    info_r = jnp.concatenate([ix[s] for s in range(n_expert)], axis=1)
+    info_c = info_r.T
+    w_in = jnp.concatenate([w_g[0], w_u[0]], axis=1)
+    gate_up = jnp.dot(tx[...], w_in, preferred_element_type=F32)
     back = jnp.dot(ox[...], w_dn[0], preferred_element_type=F32)
     gate = jnp.where(info_c[:, 0:1] == expert, info_c[:, 4:5], 0.0) + jnp.where(
         info_c[:, 2:3] == expert, info_c[:, 5:6], 0.0
@@ -323,7 +327,7 @@
         info_r[0:1, :], info_r[1:2, :], info_r[2:3, :], info_r[3:4, :], expert, n_expert, rows
     )
     hid[0] = jnp.dot(pick, grad, preferred_element_type=F32).astype(BF16)
-    term = lax.dot_general(grad, w_in[0], (((1,), (1,)), ((), ())), preferred_element_type=F32)
+    term = lax.dot_general(grad, w_in, (((1,), (1,)), ((), ())), preferred_element_type=F32)
 
     @pl.when(x == 0)
     def _():
@@ -365,7 +369,6 @@
         ],
         axis=1,
     )
-    w_in = jnp.concatenate([w_gate, w_up], axis=2)
 
     def chain_sems(number):
         return [
@@ -374,29 +377,28 @@
         ]
 
     shape = jax.ShapeDtypeStruct
-    all_in, all_dn, tx, ox, ix, tt = pl.pallas_call(
+    all_g, all_u, all_dn, tx, ox, ix, tt = pl.pallas_call(
         functools.partial(first_kernel, n_expert, n_data),
         out_shape=(
-            shape((local_count, model, 2 * hidden), BF16),
+            shape((local_count, model, hidden), BF16),
+            shape((local_count, model, hidden), BF16),
             shape((local_count, model, hidden), BF16),
             shape((n_expert, rows, model), BF16),
             shape((n_expert, rows, model), BF16),
             shape((n_expert, 8, rows), F32),
             shape((width + INFO, n_expert * n_data * rows), BF16),
         ),
-        in_specs=[vmem] * 6,
-        out_specs=[any_] * 6,
-        scratch_shapes=[dma((6,))]
-        + chain_sems(2)
+        in_specs=[vmem] * 7,
+        out_specs=[any_] * 7,
+        scratch_shapes=[dma((7,))]
+        + chain_sems(3)
         + [
             dma((3, n_expert)), dma((3, n_expert)), dma((n_data,)), dma((n_data,)),
             dma((n_expert,)), dma((n_expert,)),
         ],
         compiler_params=pltpu.CompilerParams(collective_id=0, has_side_effects=True),
-    )(w_in, w_down_t, tokens, out_grad, info, blocks)
-
-    info_r = jnp.transpose(ix, (1, 0, 2)).reshape(8, n_expert * rows)
-    info_c = info_r.T
+    )(w_gate, w_up, w_down_t, tokens, out_grad, info, blocks)
+
     total = n_expert * rows
     slots = n_expert * CAP
     hid, ret = pl.pallas_call(
@@ -406,9 +408,9 @@
         in_specs=[
             pl.BlockSpec((total, model), lambda x: (0, 0)),
             pl.BlockSpec((total, model), lambda x: (0, 0)),
-            pl.BlockSpec((8, total), lambda x: (0, 0)),
-            pl.BlockSpec((total, 8), lambda x: (0, 0)),
-            pl.BlockSpec((1, model, 2 * hidden), lambda x: (x, 0, 0)),
+            pl.BlockSpec((n_expert, 8, rows), lambda x: (0, 0, 0)),
+            pl.BlockSpec((1, model, hidden), lambda x: (x, 0, 0)),
+            pl.BlockSpec((1, model, hidden), lambda x: (x, 0, 0)),
             pl.BlockSpec((1, model, hidden), lambda x: (x, 0, 0)),
         ],
         out_specs=[
@@ -417,27 +419,30 @@
         ],
         scratch_shapes=[pltpu.VMEM((total, model), F32)],
         compiler_params=pltpu.CompilerParams(vmem_limit_bytes=60 * 1024 * 1024),
-    )(tx.reshape(total, model), ox.reshape(total, model), info_r, info_c, all_in, all_dn)
+    )(tx.reshape(total, model), ox.reshape(total, model), ix, all_g, all_u, all_dn)
 
     grad_scale = 1.0 / math.sqrt(rows * n_expert * n_data)
-    rx, grad_gate, grad_up = pl.pallas_call(
-        functools.partial(second_kernel, n_expert, n_data, grad_scale),
+    token_grad, grad_gate, grad_up = pl.pallas_call(
+        functools.partial(second_kernel, n_expert, n_data),
         out_shape=(
-            shape((n_expert, rows, model), BF16),
+            shape((rows, model), BF16),
             shape((local_count, width, hidden), F32),
             shape((local_count, width, hidden), F32),
         ),
         in_specs=[vmem] * 3,
-        out_specs=[any_, vmem, vmem],
-        scratch_shapes=[pltpu.VMEM((n_data, local_count, slots, 2 * hidden), BF16), dma((2,))]
+        out_specs=[vmem] * 3,
+        scratch_shapes=[
+            pltpu.VMEM((n_data, local_count, slots, 2 * hidden), BF16),
+            pltpu.VMEM((n_expert, rows, model), BF16),
+            dma,
+        ]
         + chain_sems(1)
         + [dma((n_expert,)), dma((n_expert,))],
         compiler_params=pltpu.CompilerParams(
             collective_id=1, has_side_effects=True, vmem_limit_bytes=60 * 1024 * 1024
         ),
     )(hid, ret.reshape(n_expert, rows, model), tt)
-    token_grad = jnp.sum(rx.astype(F32), axis=0).astype(BF16)
-    return token_grad, grad_gate, grad_up
+    return token_grad, grad_gate * grad_scale, grad_up * grad_scale
 
 
 def solution(mesh):

time: 144 us -> 130 us (0.903)
  Pallas kernels: 130 us -> 118 us
    pallas_call x1, Pallas kernels: 83.4 us -> 72.1 us  [local(): pl.pallas_call(functools.partial(first_kernel, n_expert, n_data), out_sha...]
    mul x0 -> x2, other arithmetic: none -> 3.61 us  [local(): return (token_grad, grad_gate * grad_scale, grad_up * grad_scale)]
    reduce_sum x1 -> x0, other arithmetic: 2.87 us -> none  [local(): token_grad = jnp.sum(rx.astype(F32), axis=0).astype(BF16)]
    concatenate x1 -> x0, other arithmetic: 1.82 us -> none  [local(): w_in = jnp.concatenate([w_gate, w_up], axis=2)]
where the time goes in v3:
time: 130 us
  Pallas kernels  118 us (91%)
  other arithmetic  6.25 us (5%)
  local copies, waits for them, and re-layouts  5.19 us (4%)
    pallas_call x1, Pallas kernels, local(): pl.pallas_call(functools.partial(first_kernel, n_expert, n_data), out_sha...  72.1 us
    pallas_call x1, Pallas kernels, local(): pl.pallas_call(functools.partial(second_kernel, n_expert, n_data), out_sh...  33.9 us
    pallas_call x1, Pallas kernels, local(): pl.pallas_call(functools.partial(compute_kernel, n_expert), grid=(local_c...  11.7 us
    mul x2, other arithmetic, local(): return (token_grad, grad_gate * grad_scale, grad_up * grad_scale)  3.61 us

profile of v3, /device:TPU:0, one launch (start us, length us, event | category | flops | bytes accessed | tf_op | source)
XLA Modules:
  0.0 129.8 jit_solution(16704050819319888351)
XLA Ops:
  0.6 0.8 slice_bitcast_fusion
  1.4 0.8 fusion.11
  2.1 0.8 copy.14
  2.9 0.1 eq.29
  3.1 0.1 eq.25
  3.2 0.6 reduce-window.6
  3.8 0.2 slice_reduce_fusion
  4.1 0.1 fusion.6
  4.2 0.1 reshape.86
  4.3 0.2 fusion
  4.5 0.6 stack.4.info
  5.2 1.5 %copy.16 = bf16[3072,128]{1,0:T(8,128)(2,1)S(1)} copy(bf16[3072,128]{0,1:T(8,128)(2,1)} %bitcast.27) | data formatting | bytes 1572864 | tf_op jit(solution)/shard_map/transpose | solution.py:367
  6.7 1.0 pad_maximum_fusion.blocks
  7.6 72.1 %shard_map.94 = (bf16[4,3072,128]{2,1,0:T(8,128)(2,1)}, bf16[4,3072,128]{2,1,0:T(8,128)(2,1)}, bf16[4,3072,128]{2,1,0:T(8,128)(2,1)}, bf16[2,128,3072]{2,1,0:T(8...) custom-call(bf16[4,192,128]{2,1,0:T(8,128)(2,1)} %w_g.1, ...), custom_call_target="tpu_custom_call" | custom-call | tf_op jit(solution)/shard_map/pallas_call | solution.py:380
  79.7 11.7 %shard_map.95 = (bf16[4,80,256]{2,1,0:T(8,128)(2,1)}, bf16[256,3072]{1,0:T(8,128)(2,1)}) custom-call(bf16[256,3072]{1,0:T(8,128)(2,1)} %bitcast.30, bf16[256,3072]{1,0:T(8,128)(2,1)} %bitcast.31, f32[2,8,128]{2,1,0:T(8,128)} %get-tuple-element.17.ix, bf16[4,3072,128]{2,1,0:T(8,128)(2,1)} %get-tuple-element.18.w_g, ...), custom_call_target="tpu_custom_call" | custom-call | tf_op jit(solution)/shard_map/pallas_call | solution.py:404
  91.5 33.9 %shard_map.96 = (bf16[128,3072]{1,0:T(8,128)(2,1)}, f32[4,192,128]{2,1,0:T(8,128)}, f32[4,192,128]{2,1,0:T(8,128)}) custom-call(bf16[4,80,256]{2,1,0:T(8,128)(2,1)} %get-tuple-element.21.hid, bf16[2,128,3072]{2,1,0:T(8,128)(2,1)} %bitcast.29, bf16[208,4096]{1,0:T(8,128)(2,1)} %get-tuple-element.23.tt), custom_call_target="tpu_custom_call" | custom-call | tf_op jit(solution)/shard_map/pallas_call | solution.py:425
  125.3 0.0 copy-start
  125.3 1.8 %broadcast_multiply_fusion.1 = f32[4,192,128]{2,1,0:T(8,128)} fusion(f32[4,192,128]{2,1,0:T(8,128)} %get-tuple-element.25), kind=kLoop, calls=%fused_computation.2 | loop fusion | flops 98304 | bytes 786432 | tf_op jit(solution)/shard_map/mul | solution.py:445
  127.2 1.8 %broadcast_multiply_fusion = f32[4,192,128]{2,1,0:T(8,128)} fusion(f32[4,192,128]{2,1,0:T(8,128)} %get-tuple-element.26), kind=kLoop, calls=%fused_computation.1 | loop fusion | flops 98304 | bytes 786432 | tf_op jit(solution)/shard_map/mul | solution.py:445
  129.0 0.0 copy-done
  129.0 0.9 copy.18
  (6 shorter events, 0.1 us)
Async XLA Ops:
  125.3 3.6 %copy-start = (bf16[128,3072]{1,0:T(8,128)(2,1)S(1)}, bf16[128,3072]{1,0:T(8,128)(2,1)}, u32[]{:S(2)}) copy-start(bf16[128,3072]{1,0:T(8,128)(2,1)} %get-tuple-element.40) | copy-start | bytes 2359300

commit v4 on v3

--- a/solution.py
+++ b/solution.py
@@ -237,7 +237,7 @@
 
 
 def second_kernel(
-    n_expert, n_data, hid, ret, tt, tg, out_g, out_u,
+    n_expert, n_data, scale, hid, ret, tt, tg, out_g, out_u,
     all_hid, rx, own_sem, up_s, down_s, b_s, c_s, recv, x_s, x_r,
 ):
     e, d = lax.axis_index("expert"), lax.axis_index("dp")
@@ -285,6 +285,8 @@
             out_u[x] += term[:, hidden:]
 
     gather(e, d, n_data, (hid,), block, (up_s, down_s, b_s, c_s, recv), sends, hook, use)
+    out_g[...] = out_g[...] * scale
+    out_u[...] = out_u[...] * scale
     total = ret[e].astype(F32)
     for j in range(1, n_expert):
         source = lax.rem(e - j + n_expert, n_expert)
@@ -423,7 +425,7 @@
 
     grad_scale = 1.0 / math.sqrt(rows * n_expert * n_data)
     token_grad, grad_gate, grad_up = pl.pallas_call(
-        functools.partial(second_kernel, n_expert, n_data),
+        functools.partial(second_kernel, n_expert, n_data, grad_scale),
         out_shape=(
             shape((rows, model), BF16),
             shape((local_count, width, hidden), F32),
@@ -442,7 +444,7 @@
             collective_id=1, has_side_effects=True, vmem_limit_bytes=60 * 1024 * 1024
         ),
     )(hid, ret.reshape(n_expert, rows, model), tt)
-    return token_grad, grad_gate * grad_scale, grad_up * grad_scale
+    return token_grad, grad_gate, grad_up
 
 
 def solution(mesh):

time: 130 us -> 129 us (level)
  other arithmetic: 6.25 us -> 2.64 us
  local copies, waits for them, and re-layouts: 5.19 us -> 7.94 us
    mul x2 -> x0, other arithmetic: 3.61 us -> none  [local(): return (token_grad, grad_gate * grad_scale, grad_up * grad_scale)]
    unnamed x4 -> x8, local copies, waits for them, and re-layouts: 1.67 us -> 4.42 us
where the time goes in v4:
time: 129 us
  Pallas kernels  118 us (91%)
  local copies, waits for them, and re-layouts  7.94 us (6%)
  other arithmetic  2.64 us (2%)
    pallas_call x1, Pallas kernels, local(): pl.pallas_call(functools.partial(first_kernel, n_expert, n_data), out_sha...  72.1 us
    pallas_call x1, Pallas kernels, local(): pl.pallas_call(functools.partial(second_kernel, n_expert, n_data, grad_sc...  33.9 us
    pallas_call x1, Pallas kernels, local(): pl.pallas_call(functools.partial(compute_kernel, n_expert), grid=(local_c...  11.7 us
    unnamed x8, local copies, waits for them, and re-layouts  4.42 us

profile of v4, /device:TPU:0, one launch (start us, length us, event | category | flops | bytes accessed | tf_op | source)
XLA Modules:
  0.0 129.0 jit_solution(15242996084286516020)
XLA Ops:
  0.6 0.8 slice_bitcast_fusion
  1.4 0.8 fusion.11
  2.1 0.8 copy.14
  2.9 0.1 eq.29
  3.1 0.1 eq.25
  3.2 0.6 reduce-window.6
  3.8 0.2 slice_reduce_fusion
  4.1 0.1 fusion.6
  4.2 0.1 reshape.86
  4.3 0.2 fusion
  4.5 0.6 stack.4.info
  5.2 1.5 %copy.16 = bf16[3072,128]{1,0:T(8,128)(2,1)S(1)} copy(bf16[3072,128]{0,1:T(8,128)(2,1)} %bitcast.27) | data formatting | bytes 1572864 | tf_op jit(solution)/shard_map/transpose | solution.py:369
  6.7 1.0 pad_maximum_fusion.blocks
  7.6 72.1 %shard_map.94 = (bf16[4,3072,128]{2,1,0:T(8,128)(2,1)}, bf16[4,3072,128]{2,1,0:T(8,128)(2,1)}, bf16[4,3072,128]{2,1,0:T(8,128)(2,1)}, bf16[2,128,3072]{2,1,0:T(8...) custom-call(bf16[4,192,128]{2,1,0:T(8,128)(2,1)} %w_g.1, ...), custom_call_target="tpu_custom_call" | custom-call | tf_op jit(solution)/shard_map/pallas_call | solution.py:382
  79.7 11.7 %shard_map.95 = (bf16[4,80,256]{2,1,0:T(8,128)(2,1)}, bf16[256,3072]{1,0:T(8,128)(2,1)}) custom-call(bf16[256,3072]{1,0:T(8,128)(2,1)} %bitcast.30, bf16[256,3072]{1,0:T(8,128)(2,1)} %bitcast.31, f32[2,8,128]{2,1,0:T(8,128)} %get-tuple-element.14.ix, bf16[4,3072,128]{2,1,0:T(8,128)(2,1)} %get-tuple-element.15.w_g, ...), custom_call_target="tpu_custom_call" | custom-call | tf_op jit(solution)/shard_map/pallas_call | solution.py:406
  91.5 33.9 %shard_map.96 = (bf16[128,3072]{1,0:T(8,128)(2,1)}, f32[4,192,128]{2,1,0:T(8,128)}, f32[4,192,128]{2,1,0:T(8,128)}) custom-call(bf16[4,80,256]{2,1,0:T(8,128)(2,1)} %get-tuple-element.18.hid, bf16[2,128,3072]{2,1,0:T(8,128)(2,1)} %bitcast.29, bf16[208,4096]{1,0:T(8,128)(2,1)} %get-tuple-element.20.tt), custom_call_target="tpu_custom_call" | custom-call | tf_op jit(solution)/shard_map/pallas_call | solution.py:427
  125.4 0.0 copy-start.1
  125.4 0.0 copy-start
  125.4 2.1 %copy.20 = bf16[128,3072]{1,0:T(8,128)(2,1)} copy(bf16[128,3072]{1,0:T(8,128)(2,1)} %get-tuple-element.34) | data formatting | bytes 1572864
  127.5 0.0 copy-done.1
  127.5 0.7 copy.21
  128.3 0.0 copy-done
  128.3 0.7 copy.22
  (6 shorter events, 0.1 us)
Async XLA Ops:
  125.4 2.2 %copy-start.1 = (f32[4,192,128]{2,1,0:T(8,128)S(1)}, f32[4,192,128]{2,1,0:T(8,128)}, u32[]{:S(2)}) copy-start(f32[4,192,128]{2,1,0:T(8,128)} %get-tuple-element.35) | copy-start | bytes 1179652
  125.4 2.9 %copy-start = (f32[4,192,128]{2,1,0:T(8,128)S(1)}, f32[4,192,128]{2,1,0:T(8,128)}, u32[]{:S(2)}) copy-start(f32[4,192,128]{2,1,0:T(8,128)} %get-tuple-element.36) | copy-start | bytes 1179652
